TPU v7x, 32 devices: a whole 2x2x4 slice. The times are simulated.
32 devices in a mesh: gx: 8 (over y, x, core), gy: 4 (over z).
Axes of the slice: x: 2, y: 2, z: 4, core: 2. Of those that a mesh axis runs over, the one named last changes fastest.
Arguments:
- displacement: float32 [3, 128, 128, 128], P(None, 'gx', 'gy'), may hold values from -4 to 4
- force: float32 [3, 128, 128, 128], P(None, 'gx', 'gy'), may hold values from -12 to 12
- damage: float32 [128, 128, 128], P('gx', 'gy'), may hold values from 0 to 0.8
- history: float32 [128, 128, 128], P('gx', 'gy'), may hold values from 0.05 to 3
- crack_flags: int32 [128, 128, 128], P('gx', 'gy'), may hold values 0 or 1
Outputs:
- displacement_out: float32 [3, 128, 128, 128], P(None, 'gx', 'gy')
- damage_out: float32 [128, 128, 128], P('gx', 'gy')
- history_out: float32 [128, 128, 128], P('gx', 'gy')
All inputs are finite; a program needn't handle non-finite values. No bound on the sum of `crack_flags` on one device may be relied on, other than what follows from the above.
Results may differ from a plain program's by a relative error of at most 0.0003.
Values sent between devices are 32-bit elements; how exact they have to be, the bound alone decides.
A program may use at most 64 MiB of HBM per device.

v0:
```python
import jax
import jax.numpy as jnp
from jax import lax
from jax.sharding import PartitionSpec as P

ITERS = 3


shear_modulus = 1.0
lame_first = 1.5
spring_term = 0.5
stiff_floor = 0.001
crack_load = 4.0
tough_ratio = 0.5
length_term = 2.0
stress_index = ((0, 3, 4), (3, 1, 5), (4, 5, 2))


def padded_2(shard, sides, width):
    for axis, dim in sides:
        size, length = (lax.axis_size(axis), shard.shape[dim])
        up = [(i, (i + 1) % size) for i in range(size - 1)]
        down = [(j, i) for i, j in up]
        last = lax.slice_in_dim(shard, length - width, length, axis=dim)
        leading = lax.slice_in_dim(shard, 0, width, axis=dim)
        before = lax.ppermute(last, axis, up)
        after = lax.ppermute(leading, axis, down)
        shard = jnp.concatenate([before, shard, after], axis=dim)
    return shard


def strains(padded):
    base = padded[:, :-1, :-1, :-1]
    grads = []
    for component in range(3):
        grads.append(
            (
                padded[component, 1:, :-1, :-1] - base[component],
                padded[component, :-1, 1:, :-1] - base[component],
                padded[component, :-1, :-1, 1:] - base[component],
            )
        )
    return (
        grads[0][0],
        grads[1][1],
        grads[2][2],
        0.5 * (grads[0][1] + grads[1][0]),
        0.5 * (grads[0][2] + grads[2][0]),
        0.5 * (grads[1][2] + grads[2][1]),
    )


def lowered(values, direction):
    if direction == 0:
        return values[:-1, 1:, 1:]
    if direction == 1:
        return values[1:, :-1, 1:]
    return values[1:, 1:, :-1]


def elastic(padded, padded_gain):
    strain = strains(padded)
    weight = padded_gain[:-1, :-1, :-1]
    trace = strain[0] + strain[1] + strain[2]
    stress = [
        weight * (2.0 * shear_modulus * strain[index] + lame_first * trace) for index in range(3)
    ]
    stress = stress + [weight * (2.0 * shear_modulus * strain[index]) for index in range(3, 6)]
    images = []
    for component in range(3):
        summed = spring_term * padded[component, 1:-1, 1:-1, 1:-1]
        for direction in range(3):
            values = stress[stress_index[component][direction]]
            summed = summed + lowered(values, direction) - values[1:, 1:, 1:]
        images.append(summed)
    return (jnp.stack(images), strain)


def energy(strain):
    owned = [item[1:, 1:, 1:] for item in strain]
    trace = owned[0] + owned[1] + owned[2]
    squares = (
        owned[0] ** 2
        + owned[1] ** 2
        + owned[2] ** 2
        + 2.0 * (owned[3] ** 2 + owned[4] ** 2 + owned[5] ** 2)
    )
    bulk_half = 0.5 * (lame_first + 2.0 * shear_modulus / 3.0)
    return bulk_half * jnp.maximum(trace, 0.0) ** 2 + shear_modulus * (
        squares - trace * trace / 3.0
    )


def damage_apply(padded, driving):
    center = padded[1:-1, 1:-1, 1:-1]
    beside_all = (
        padded[2:, 1:-1, 1:-1]
        + padded[:-2, 1:-1, 1:-1]
        + padded[1:-1, 2:, 1:-1]
        + padded[1:-1, :-2, 1:-1]
        + padded[1:-1, 1:-1, 2:]
        + padded[1:-1, 1:-1, :-2]
    )
    return (tough_ratio + 2.0 * driving) * center + length_term * (6.0 * center - beside_all)


def pad_depth(values):
    widths = [(0, 0)] * (values.ndim - 1) + [(1, 1)]
    return jnp.pad(values, widths)


def vector_rim(values):
    extended = padded_2(values, (("gx", 1), ("gy", 2)), 1)
    return pad_depth(extended)


def scalar_rim(values):
    extended = padded_2(values, (("gx", 0), ("gy", 1)), 1)
    return pad_depth(extended)


def paired_sums(resid, image):
    return lax.psum((jnp.sum(resid * resid), jnp.sum(resid * image)), ("gx", "gy"))


def add_scaled(first, second, factor):
    return jax.tree.map(lambda left, right: left + factor * right, first, second)


def solve(operate, start, target, first):
    current = start
    image_start, aside_now = first
    resid = target - image_start
    image, aside_resid = operate(resid)
    norm_now, product = paired_sums(resid, image)
    alpha = norm_now / product
    direction, along, aside_dir = (resid, image, aside_resid)
    for number in range(ITERS):
        current = current + alpha * direction
        aside_now = add_scaled(aside_now, aside_dir, alpha)
        resid = resid - alpha * along
        if number + 1 < ITERS:
            image, aside_resid = operate(resid)
            norm_next, product = paired_sums(resid, image)
            ratio = norm_next / norm_now
            alpha = norm_next / (product - ratio * norm_next / alpha)
            direction = resid + ratio * direction
            along = image + ratio * along
            aside_dir = add_scaled(aside_resid, aside_dir, ratio)
            norm_now = norm_next
    return (current, aside_now)


def body(displacement, force, damage, history, crack_flags):
    gain = (1.0 - damage) ** 2 + stiff_floor
    stacked = padded_2(jnp.stack([gain, damage]), (("gx", 1), ("gy", 2)), 1)
    padded_gain = pad_depth(stacked[0])
    padded_damage = pad_depth(stacked[1])

    def elastic_step(values):
        image, strain = elastic(vector_rim(values), padded_gain)
        return (image, ())

    moved, strain = solve(elastic_step, displacement, force, elastic_step(displacement))
    strain = elastic(vector_rim(moved), padded_gain)[1]
    psi = energy(strain)
    history_out = jnp.maximum(
        jnp.maximum(history, psi), crack_load * crack_flags.astype(jnp.float32)
    )

    def damage_step(values):
        return (damage_apply(scalar_rim(values), history_out), ())

    first_damage = (damage_apply(padded_damage, history_out), ())
    damage_out, unused = solve(damage_step, damage, 2.0 * history_out, first_damage)
    return (moved, damage_out, history_out)


def solution(mesh):
    return jax.shard_map(
        body,
        mesh=mesh,
        in_specs=(
            P(None, "gx", "gy", None),
            P(None, "gx", "gy", None),
            P("gx", "gy", None),
            P("gx", "gy", None),
            P("gx", "gy", None),
        ),
        out_specs=(P(None, "gx", "gy", None), P("gx", "gy", None), P("gx", "gy", None)),
        check_vma=False,
    )
```

profile of v0, /device:TPU:0, one launch (start us, length us, event | category | flops | bytes accessed | tf_op | source)
XLA Modules:
  0.0 437.6 jit_solution(12208365551340709455)
XLA Ops:
  2.5 2.4 collective-permute-start
  4.9 1.3 collective-permute-start.1
  8.3 5.8 %collective-permute-start.4 = (f32[3,1,32,128]{3,2,1,0:T(8,128)S(1)}, f32[3,1,32,128]{3,2,1,0:T(8,128)S(1)}, u32[]{:S(2)}, u32[]{:S(2)}) collective-permute-start(f32[3,1,32,128]{3,2,1,0:T(8,128)S(1)} %get-tuple-element.100), channel_id=1, source_target_pairs={{0,4},{4,8},{8,12},{12,16},{16,20},{20,24},{24,28},{1,5},{5,9},{9,... | collective-permute-start | bytes 147464 | tf_op jit(solution)/shard_map/ppermute | solution.py:26
  15.0 3.5 collective-permute-start.2
  18.5 1.3 collective-permute-start.3
  19.9 4.5 %collective-permute-start.6 = (f32[3,18,1,128]{3,2,1,0:T(1,128)S(1)}, f32[3,18,1,128]{3,2,1,0:T(1,128)S(1)}, u32[]{:S(2)}, u32[]{:S(2)}) collective-permute-start(f32[3,18,1,128]{3,2,1,0:T(1,128)S(1)} %get-tuple-element.89), channel_id=1, source_target_pairs={{0,1},{1,2},{2,3},{4,5},{5,6},{6,7},{8,9},{9,10},{10,11},{12,13},{... | collective-permute-start | bytes 82952 | tf_op jit(solution)/shard_map/ppermute | solution.py:26
  24.5 1.3 collective-permute-start.7
  26.0 4.4 %collective-permute-done.7 = f32[3,18,1,128]{3,2,1,0:T(1,128)S(1)} collective-permute-done((f32[3,18,1,128]{3,2,1,0:T(1,128)S(1)}, f32[3,18,1,128]{3,2,1,0:T(1,128)S(1)}, u32[]{:S(2)}, u32[]{:S(2)}) %collective-permute-start.7) | collective-permute-done | bytes 27680 | tf_op jit(solution)/shard_map/ppermute | solution.py:27
  35.1 1.9 collective-permute-start.8
  37.0 1.3 collective-permute-start.9
  38.3 3.4 collective-permute-done.9
  41.8 3.5 collective-permute-start.10
  45.3 1.3 collective-permute-start.11
  46.8 4.2 collective-permute-done.11
  56.1 42.0 %all-reduce.15 = (f32[]{:T(128)}, f32[]{:T(128)}) all-reduce(f32[]{:T(128)} %get-tuple-element.8, f32[]{:T(128)} %get-tuple-element.7), channel_id=1, replica_groups=mesh['gx'=8,'gy'=4] {'gx','gy'}, use_global_device_ids=true, to_apply=%region_1.2 | all-reduce | flops 2 | bytes 16 | tf_op jit(solution)/shard_map/psum | solution.py:123
  99.6 1.3 collective-permute-start.12
  102.2 4.3 collective-permute-done.13
  106.6 2.3 collective-permute-start.14
  108.9 1.5 collective-permute-start.15
  110.5 4.2 collective-permute-done.15
  119.9 41.5 %all-reduce.14 = (f32[]{:T(128)}, f32[]{:T(128)}) all-reduce(f32[]{:T(128)} %get-tuple-element.6, f32[]{:T(128)} %get-tuple-element.5), channel_id=1, replica_groups=mesh['gx'=8,'gy'=4] {'gx','gy'}, use_global_device_ids=true, to_apply=%region_5.6 | all-reduce | flops 2 | bytes 16 | tf_op jit(solution)/shard_map/psum | solution.py:123
  165.8 1.5 multiply_subtract_fusion
  169.9 4.3 collective-permute-done.17
  174.3 3.1 collective-permute-start.18
  178.9 4.2 collective-permute-done.19
  187.6 1.3 fusion.1
  188.9 40.8 %all-reduce.13 = (f32[]{:T(128)}, f32[]{:T(128)}) all-reduce(f32[]{:T(128)} %get-tuple-element.4, f32[]{:T(128)} %get-tuple-element.3), channel_id=1, replica_groups=mesh['gx'=8,'gy'=4] {'gx','gy'}, use_global_device_ids=true, to_apply=%region_9.10 | all-reduce | flops 2 | bytes 16 | tf_op jit(solution)/shard_map/psum | solution.py:123
  233.6 1.8 multiply_add_fusion
  236.7 1.5 collective-permute-start.21
  238.2 4.1 collective-permute-done.21
  242.4 3.1 collective-permute-start.22
  247.0 4.2 collective-permute-done.23
  253.9 3.3 collective-permute-start.25
  258.5 2.7 collective-permute-done.24
  261.2 2.6 collective-permute-start.27
  265.1 4.2 collective-permute-done.26
  270.5 42.1 %all-reduce.12 = (f32[]{:T(128)}, f32[]{:T(128)}) all-reduce(f32[]{:T(128)} %get-tuple-element.14, f32[]{:T(128)} %get-tuple-element.13), channel_id=1, replica_groups=mesh['gx'=8,'gy'=4] {'gx','gy'}, use_global_device_ids=true, to_apply=%region_13.14 | all-reduce | flops 2 | bytes 16 | tf_op jit(solution)/shard_map/psum | solution.py:123
  315.3 1.3 collective-permute-start.28
  316.6 4.3 collective-permute-done.28
  320.9 2.3 collective-permute-start.31
  324.5 4.2 collective-permute-done.30
  329.9 41.3 %all-reduce.11 = (f32[]{:T(128)}, f32[]{:T(128)}) all-reduce(f32[]{:T(128)} %get-tuple-element.12, f32[]{:T(128)} %get-tuple-element.11), channel_id=1, replica_groups=mesh['gx'=8,'gy'=4] {'gx','gy'}, use_global_device_ids=true, to_apply=%region_17.18 | all-reduce | flops 2 | bytes 16 | tf_op jit(solution)/shard_map/psum | solution.py:123
  377.0 1.3 collective-permute-start.32
  378.3 4.3 collective-permute-done.32
  382.6 3.1 collective-permute-start.35
  385.7 1.3 collective-permute-start.34
  387.0 4.2 collective-permute-done.34
  392.5 40.4 %all-reduce.10 = (f32[]{:T(128)}, f32[]{:T(128)}) all-reduce(f32[]{:T(128)} %get-tuple-element.10, f32[]{:T(128)} %get-tuple-element.9), channel_id=1, replica_groups=mesh['gx'=8,'gy'=4] {'gx','gy'}, use_global_device_ids=true, to_apply=%region_21.22 | all-reduce | flops 2 | bytes 16 | tf_op jit(solution)/shard_map/psum | solution.py:123
  (119 shorter events, 47.2 us)
Async XLA Ops:
  0.6 25.2 %copy-start.3 = (f32[16,32,128]{2,1,0:T(8,128)S(1)}, f32[16,32,128]{2,1,0:T(8,128)}, u32[]{:S(2)}) copy-start(f32[16,32,128]{2,1,0:T(8,128)} %param.7) | copy-start | bytes 786436
  0.6 19.2 %copy-start.1 = (f32[3,16,32,128]{3,2,1,0:T(8,128)S(1)}, f32[3,16,32,128]{3,2,1,0:T(8,128)}, u32[]{:S(2)}) copy-start(f32[3,16,32,128]{3,2,1,0:T(8,128)} %param.5) | copy-start | bytes 2359300
  2.5 11.6 %collective-permute-start = (f32[2,1,32,128]{3,2,1,0:T(8,128)S(1)}, f32[2,1,32,128]{3,2,1,0:T(8,128)S(1)}, u32[]{:S(2)}, u32[]{:S(2)}) collective-permute-start(f32[2,1,32,128]{3,2,1,0:T(8,128)S(1)} %get-tuple-element.105), channel_id=1, source_target_pairs={{0,4},{4,8},{8,12},{12,16},{16,20},{20,24},{24,28},{1,5},{5,9},{9,... | collective-permute-start | bytes 98312 | tf_op jit(solution)/shard_map/ppermute | solution.py:26
  4.9 9.2 %collective-permute-start.1 = (f32[2,1,32,128]{3,2,1,0:T(8,128)S(1)}, f32[2,1,32,128]{3,2,1,0:T(8,128)S(1)}, u32[]{:S(2)}, u32[]{:S(2)}) collective-permute-start(f32[2,1,32,128]{3,2,1,0:T(8,128)S(1)} %get-tuple-element.106), channel_id=1, source_target_pairs={{4,0},{8,4},{12,8},{16,12},{20,16},{24,20},{28,24},{5,1},{9,5},{13... | collective-permute-start | bytes 98312 | tf_op jit(solution)/shard_map/ppermute | solution.py:27
  7.0 12.9 %collective-permute-start.5 = (f32[3,1,32,128]{3,2,1,0:T(8,128)S(1)}, f32[3,1,32,128]{3,2,1,0:T(8,128)S(1)}, u32[]{:S(2)}, u32[]{:S(2)}) collective-permute-start(f32[3,1,32,128]{3,2,1,0:T(8,128)S(1)} %get-tuple-element.99), channel_id=1, source_target_pairs={{4,0},{8,4},{12,8},{16,12},{20,16},{24,20},{28,24},{5,1},{9,5},{13... | collective-permute-start | bytes 147464 | tf_op jit(solution)/shard_map/ppermute | solution.py:27
  8.3 11.5 %collective-permute-start.4 = (f32[3,1,32,128]{3,2,1,0:T(8,128)S(1)}, f32[3,1,32,128]{3,2,1,0:T(8,128)S(1)}, u32[]{:S(2)}, u32[]{:S(2)}) collective-permute-start(f32[3,1,32,128]{3,2,1,0:T(8,128)S(1)} %get-tuple-element.100), channel_id=1, source_target_pairs={{0,4},{4,8},{8,12},{12,16},{16,20},{20,24},{24,28},{1,5},{5,9},{9,... | collective-permute-start | bytes 147464 | tf_op jit(solution)/shard_map/ppermute | solution.py:26
  15.0 10.8 %collective-permute-start.2 = (f32[2,18,1,128]{3,2,1,0:T(1,128)S(1)}, f32[2,18,1,128]{3,2,1,0:T(1,128)S(1)}, u32[]{:S(2)}, u32[]{:S(2)}) collective-permute-start(f32[2,18,1,128]{3,2,1,0:T(1,128)S(1)} %get-tuple-element.103), channel_id=1, source_target_pairs={{0,1},{1,2},{2,3},{4,5},{5,6},{6,7},{8,9},{9,10},{10,11},{12,13},{... | collective-permute-start | bytes 55304 | tf_op jit(solution)/shard_map/ppermute | solution.py:26
  18.5 7.3 %collective-permute-start.3 = (f32[2,18,1,128]{3,2,1,0:T(1,128)S(1)}, f32[2,18,1,128]{3,2,1,0:T(1,128)S(1)}, u32[]{:S(2)}, u32[]{:S(2)}) collective-permute-start(f32[2,18,1,128]{3,2,1,0:T(1,128)S(1)} %get-tuple-element.104), channel_id=1, source_target_pairs={{1,0},{2,1},{3,2},{5,4},{6,5},{7,6},{9,8},{10,9},{11,10},{13,12},{... | collective-permute-start | bytes 55304 | tf_op jit(solution)/shard_map/ppermute | solution.py:27
  19.9 6.1 %collective-permute-start.6 = (f32[3,18,1,128]{3,2,1,0:T(1,128)S(1)}, f32[3,18,1,128]{3,2,1,0:T(1,128)S(1)}, u32[]{:S(2)}, u32[]{:S(2)}) collective-permute-start(f32[3,18,1,128]{3,2,1,0:T(1,128)S(1)} %get-tuple-element.89), channel_id=1, source_target_pairs={{0,1},{1,2},{2,3},{4,5},{5,6},{6,7},{8,9},{9,10},{10,11},{12,13},{... | collective-permute-start | bytes 82952 | tf_op jit(solution)/shard_map/ppermute | solution.py:26
  24.5 6.0 %collective-permute-start.7 = (f32[3,18,1,128]{3,2,1,0:T(1,128)S(1)}, f32[3,18,1,128]{3,2,1,0:T(1,128)S(1)}, u32[]{:S(2)}, u32[]{:S(2)}) collective-permute-start(f32[3,18,1,128]{3,2,1,0:T(1,128)S(1)} %get-tuple-element.90), channel_id=1, source_target_pairs={{1,0},{2,1},{3,2},{5,4},{6,5},{7,6},{9,8},{10,9},{11,10},{13,12},{... | collective-permute-start | bytes 82952 | tf_op jit(solution)/shard_map/ppermute | solution.py:27
  33.8 1.1 copy-start
  35.1 3.3 collective-permute-start.8
  37.0 4.7 %collective-permute-start.9 = (f32[3,1,32,128]{3,2,1,0:T(8,128)S(1)}, f32[3,1,32,128]{3,2,1,0:T(8,128)S(1)}, u32[]{:S(2)}, u32[]{:S(2)}) collective-permute-start(f32[3,1,32,128]{3,2,1,0:T(8,128)S(1)} %get-tuple-element.98), channel_id=1, source_target_pairs={{4,0},{8,4},{12,8},{16,12},{20,16},{24,20},{28,24},{5,1},{9,5},{13... | collective-permute-start | bytes 147464 | tf_op jit(solution)/shard_map/ppermute | solution.py:27
  41.8 5.0 %collective-permute-start.10 = (f32[3,18,1,128]{3,2,1,0:T(1,128)S(1)}, f32[3,18,1,128]{3,2,1,0:T(1,128)S(1)}, u32[]{:S(2)}, u32[]{:S(2)}) collective-permute-start(f32[3,18,1,128]{3,2,1,0:T(1,128)S(1)} %get-tuple-element.87), channel_id=1, source_target_pairs={{0,1},{1,2},{2,3},{4,5},{5,6},{6,7},{8,9},{9,10},{10,11},{12,13},{... | collective-permute-start | bytes 82952 | tf_op jit(solution)/shard_map/ppermute | solution.py:26
  45.3 5.8 %collective-permute-start.11 = (f32[3,18,1,128]{3,2,1,0:T(1,128)S(1)}, f32[3,18,1,128]{3,2,1,0:T(1,128)S(1)}, u32[]{:S(2)}, u32[]{:S(2)}) collective-permute-start(f32[3,18,1,128]{3,2,1,0:T(1,128)S(1)} %get-tuple-element.88), channel_id=1, source_target_pairs={{1,0},{2,1},{3,2},{5,4},{6,5},{7,6},{9,8},{10,9},{11,10},{13,12},{... | collective-permute-start | bytes 82952 | tf_op jit(solution)/shard_map/ppermute | solution.py:27
  99.6 2.6 collective-permute-start.12
  100.9 5.6 %collective-permute-start.13 = (f32[3,1,32,128]{3,2,1,0:T(8,128)S(1)}, f32[3,1,32,128]{3,2,1,0:T(8,128)S(1)}, u32[]{:S(2)}, u32[]{:S(2)}) collective-permute-start(f32[3,1,32,128]{3,2,1,0:T(8,128)S(1)} %get-tuple-element.96), channel_id=1, source_target_pairs={{4,0},{8,4},{12,8},{16,12},{20,16},{24,20},{28,24},{5,1},{9,5},{13... | collective-permute-start | bytes 147464 | tf_op jit(solution)/shard_map/ppermute | solution.py:27
  106.6 3.8 collective-permute-start.14
  108.9 5.8 %collective-permute-start.15 = (f32[3,18,1,128]{3,2,1,0:T(1,128)S(1)}, f32[3,18,1,128]{3,2,1,0:T(1,128)S(1)}, u32[]{:S(2)}, u32[]{:S(2)}) collective-permute-start(f32[3,18,1,128]{3,2,1,0:T(1,128)S(1)} %get-tuple-element.86), channel_id=1, source_target_pairs={{1,0},{2,1},{3,2},{5,4},{6,5},{7,6},{9,8},{10,9},{11,10},{13,12},{... | collective-permute-start | bytes 82952 | tf_op jit(solution)/shard_map/ppermute | solution.py:27
  118.0 1.9 copy-start.4
  118.8 1.2 copy-start.6
  118.8 1.2 copy-start.8
  167.3 2.6 collective-permute-start.16
  168.6 5.6 %collective-permute-start.17 = (f32[3,1,32,128]{3,2,1,0:T(8,128)S(1)}, f32[3,1,32,128]{3,2,1,0:T(8,128)S(1)}, u32[]{:S(2)}, u32[]{:S(2)}) collective-permute-start(f32[3,1,32,128]{3,2,1,0:T(8,128)S(1)} %get-tuple-element.94), channel_id=1, source_target_pairs={{4,0},{8,4},{12,8},{16,12},{20,16},{24,20},{28,24},{5,1},{9,5},{13... | collective-permute-start | bytes 147464 | tf_op jit(solution)/shard_map/ppermute | solution.py:27
  174.3 4.6 %collective-permute-start.18 = (f32[3,18,1,128]{3,2,1,0:T(1,128)S(1)}, f32[3,18,1,128]{3,2,1,0:T(1,128)S(1)}, u32[]{:S(2)}, u32[]{:S(2)}) collective-permute-start(f32[3,18,1,128]{3,2,1,0:T(1,128)S(1)} %get-tuple-element.83), channel_id=1, source_target_pairs={{0,1},{1,2},{2,3},{4,5},{5,6},{6,7},{8,9},{9,10},{10,11},{12,13},{... | collective-permute-start | bytes 82952 | tf_op jit(solution)/shard_map/ppermute | solution.py:26
  177.4 5.8 %collective-permute-start.19 = (f32[3,18,1,128]{3,2,1,0:T(1,128)S(1)}, f32[3,18,1,128]{3,2,1,0:T(1,128)S(1)}, u32[]{:S(2)}, u32[]{:S(2)}) collective-permute-start(f32[3,18,1,128]{3,2,1,0:T(1,128)S(1)} %get-tuple-element.84), channel_id=1, source_target_pairs={{1,0},{2,1},{3,2},{5,4},{6,5},{7,6},{9,8},{10,9},{11,10},{13,12},{... | collective-permute-start | bytes 82952 | tf_op jit(solution)/shard_map/ppermute | solution.py:27
  186.4 1.0 copy-start.5
  186.5 1.0 copy-start.7
  186.5 1.1 copy-start.9
  235.4 15.8 %copy-start.2 = (f32[3,16,32,128]{3,2,1,0:T(8,128)}, f32[3,16,32,128]{3,2,1,0:T(8,128)S(1)}, u32[]{:S(2)}) copy-start(f32[3,16,32,128]{3,2,1,0:T(8,128)S(1)} %multiply_add_fusion) | copy-start | bytes 2359300
  235.4 2.8 collective-permute-start.20
  236.7 5.6 %collective-permute-start.21 = (f32[3,1,32,128]{3,2,1,0:T(8,128)S(1)}, f32[3,1,32,128]{3,2,1,0:T(8,128)S(1)}, u32[]{:S(2)}, u32[]{:S(2)}) collective-permute-start(f32[3,1,32,128]{3,2,1,0:T(8,128)S(1)} %get-tuple-element.92), channel_id=1, source_target_pairs={{4,0},{8,4},{12,8},{16,12},{20,16},{24,20},{28,24},{5,1},{9,5},{13... | collective-permute-start | bytes 147464 | tf_op jit(solution)/shard_map/ppermute | solution.py:27
  242.4 4.6 %collective-permute-start.22 = (f32[3,18,1,128]{3,2,1,0:T(1,128)S(1)}, f32[3,18,1,128]{3,2,1,0:T(1,128)S(1)}, u32[]{:S(2)}, u32[]{:S(2)}) collective-permute-start(f32[3,18,1,128]{3,2,1,0:T(1,128)S(1)} %get-tuple-element.81), channel_id=1, source_target_pairs={{0,1},{1,2},{2,3},{4,5},{5,6},{6,7},{8,9},{9,10},{10,11},{12,13},{... | collective-permute-start | bytes 82952 | tf_op jit(solution)/shard_map/ppermute | solution.py:26
  245.4 5.8 %collective-permute-start.23 = (f32[3,18,1,128]{3,2,1,0:T(1,128)S(1)}, f32[3,18,1,128]{3,2,1,0:T(1,128)S(1)}, u32[]{:S(2)}, u32[]{:S(2)}) collective-permute-start(f32[3,18,1,128]{3,2,1,0:T(1,128)S(1)} %get-tuple-element.82), channel_id=1, source_target_pairs={{1,0},{2,1},{3,2},{5,4},{6,5},{7,6},{9,8},{10,9},{11,10},{13,12},{... | collective-permute-start | bytes 82952 | tf_op jit(solution)/shard_map/ppermute | solution.py:27
  252.1 1.0 copy-start.12
  253.9 137.7 %copy-start.10 = (f32[16,32,128]{2,1,0:T(8,128)}, f32[16,32,128]{2,1,0:T(8,128)S(1)}, u32[]{:S(2)}) copy-start(f32[16,32,128]{2,1,0:T(8,128)S(1)} %get-tuple-element.30) | copy-start | bytes 786436
  253.9 4.6 %collective-permute-start.25 = (f32[1,32,128]{2,1,0:T(8,128)S(1)}, f32[1,32,128]{2,1,0:T(8,128)S(1)}, u32[]{:S(2)}, u32[]{:S(2)}) collective-permute-start(f32[1,32,128]{2,1,0:T(8,128)S(1)} %get-tuple-element.117), channel_id=1, source_target_pairs={{0,4},{4,8},{8,12},{12,16},{16,20},{20,24},{24,28},{1,5},{5,9},{9,... | collective-permute-start | bytes 49160 | tf_op jit(solution)/shard_map/ppermute | solution.py:26
  257.2 4.0 collective-permute-start.24
  261.2 3.9 collective-permute-start.27
  263.7 5.6 %collective-permute-start.26 = (f32[18,1,128]{2,1,0:T(1,128)S(1)}, f32[18,1,128]{2,1,0:T(1,128)S(1)}, u32[]{:S(2)}, u32[]{:S(2)}) collective-permute-start(f32[18,1,128]{2,1,0:T(1,128)S(1)} %get-tuple-element.112), channel_id=1, source_target_pairs={{1,0},{2,1},{3,2},{5,4},{6,5},{7,6},{9,8},{10,9},{11,10},{13,12},{... | collective-permute-start | bytes 27656 | tf_op jit(solution)/shard_map/ppermute | solution.py:27
  314.0 2.6 collective-permute-start.29
  315.3 5.6 %collective-permute-start.28 = (f32[1,32,128]{2,1,0:T(8,128)S(1)}, f32[1,32,128]{2,1,0:T(8,128)S(1)}, u32[]{:S(2)}, u32[]{:S(2)}) collective-permute-start(f32[1,32,128]{2,1,0:T(8,128)S(1)} %get-tuple-element.116), channel_id=1, source_target_pairs={{4,0},{8,4},{12,8},{16,12},{20,16},{24,20},{28,24},{5,1},{9,5},{13... | collective-permute-start | bytes 49160 | tf_op jit(solution)/shard_map/ppermute | solution.py:27
  320.9 3.6 collective-permute-start.31
  323.1 5.6 %collective-permute-start.30 = (f32[18,1,128]{2,1,0:T(1,128)S(1)}, f32[18,1,128]{2,1,0:T(1,128)S(1)}, u32[]{:S(2)}, u32[]{:S(2)}) collective-permute-start(f32[18,1,128]{2,1,0:T(1,128)S(1)} %get-tuple-element.110), channel_id=1, source_target_pairs={{1,0},{2,1},{3,2},{5,4},{6,5},{7,6},{9,8},{10,9},{11,10},{13,12},{... | collective-permute-start | bytes 27656 | tf_op jit(solution)/shard_map/ppermute | solution.py:27
  375.7 2.6 collective-permute-start.33
  377.0 5.6 %collective-permute-start.32 = (f32[1,32,128]{2,1,0:T(8,128)S(1)}, f32[1,32,128]{2,1,0:T(8,128)S(1)}, u32[]{:S(2)}, u32[]{:S(2)}) collective-permute-start(f32[1,32,128]{2,1,0:T(8,128)S(1)} %get-tuple-element.114), channel_id=1, source_target_pairs={{4,0},{8,4},{12,8},{16,12},{20,16},{24,20},{28,24},{5,1},{9,5},{13... | collective-permute-start | bytes 49160 | tf_op jit(solution)/shard_map/ppermute | solution.py:27
  382.6 4.4 %collective-permute-start.35 = (f32[18,1,128]{2,1,0:T(1,128)S(1)}, f32[18,1,128]{2,1,0:T(1,128)S(1)}, u32[]{:S(2)}, u32[]{:S(2)}) collective-permute-start(f32[18,1,128]{2,1,0:T(1,128)S(1)} %get-tuple-element.107), channel_id=1, source_target_pairs={{0,1},{1,2},{2,3},{4,5},{5,6},{6,7},{8,9},{9,10},{10,11},{12,13},{... | collective-permute-start | bytes 27656 | tf_op jit(solution)/shard_map/ppermute | solution.py:26
  385.7 5.6 %collective-permute-start.34 = (f32[18,1,128]{2,1,0:T(1,128)S(1)}, f32[18,1,128]{2,1,0:T(1,128)S(1)}, u32[]{:S(2)}, u32[]{:S(2)}) collective-permute-start(f32[18,1,128]{2,1,0:T(1,128)S(1)} %get-tuple-element.108), channel_id=1, source_target_pairs={{1,0},{2,1},{3,2},{5,4},{6,5},{7,6},{9,8},{10,9},{11,10},{13,12},{... | collective-permute-start | bytes 27656 | tf_op jit(solution)/shard_map/ppermute | solution.py:27
  (1 other events, 1.0 us)
where the time goes:
time: 440 us; the launch traced here: 438 us
  blocking collectives  248 us (56%)
  starting transfers between devices  71.3 us (16%)
  waiting for transfers between devices  62.3 us (14%)
  other arithmetic  33.1 us (8%)
  between operations  20.7 us (5%)
    psum x6, blocking collectives, paired_sums(): lax.psum((jnp.sum(resid * resid), jnp.sum(resid * image)), ('gx', 'gy'))  248 us
    ppermute x18, waiting for transfers between devices, padded_2(): after = lax.ppermute(leading, axis, down)  61.3 us
    ppermute x18, starting transfers between devices, padded_2(): before = lax.ppermute(last, axis, up)  47.6 us
    ppermute x18, starting transfers between devices, padded_2(): after = lax.ppermute(leading, axis, down)  23.6 us
  transfers between devices with their start and end apart: 36, of which 21 were waited for; matrix products, arithmetic and copies ran while one was open for 0% of the time, Pallas kernels for 0%

commit v1 on v0

v1 whole, which is shorter than its diff:
```python
import functools
import jax
import jax.numpy as jnp
from jax import lax
from jax.experimental import pallas as pl
from jax.experimental.pallas import tpu as pltpu
from jax.sharding import PartitionSpec as P

XO = 2
XF = 3
RO = 8
DIRS = ((1, 0), (-1, 0), (0, 1), (0, -1), (1, 1), (1, -1), (-1, 1), (-1, -1))
MESH = pl.DeviceIdType.MESH
U_EX, D_EX, R_EX, W_EX, H_EX = range(5)
WIDTHS = {
    U_EX: (3, 1, 1, 1, 1),
    D_EX: (1, 2, 2, 2, 2),
    R_EX: (3, 2, 3, 2, 4),
    W_EX: (1, 2, 3, 2, 4),
    H_EX: (1, 1, 2, 1, 2),
}


def galerkin(total):
    m = [total[k : k + 1, :] for k in range(6)]
    l10, l20 = m[2] / m[1], m[3] / m[1]
    d1 = m[3] - l10 * m[2]
    e1 = m[4] - l20 * m[2]
    l21 = e1 / d1
    f1 = m[5] - l20 * m[3] - l21 * e1
    z1 = m[1] - l10 * m[0]
    z2 = m[2] - l20 * m[0] - l21 * z1
    y2 = jnp.where(f1 > 0.0, z2 / f1, 0.0)
    y1 = jnp.where(d1 > 0.0, z1 / d1 - l21 * y2, 0.0)
    y2 = jnp.where(d1 > 0.0, y2, 0.0)
    y0 = m[0] / m[1] - l10 * y1 - l20 * y2
    y0 = jnp.where(d1 > 0.0, y0, m[0] / m[1])
    return y0, y1, y2


def kernel(sizes, u_in, f_in, d_in, hist_in, crack_in, u_out, d_out, h_out, *scratch):
    n_gx, n_gy, X, Y, Z = sizes
    (U, V0, V1, V2, S, G, D, H, W0, W1, W2, F, HI, CR) = scratch[:14]
    stages = scratch[14:34]
    part, gath, send_sem, recv_sem, ar_send, ar_recv, loc_sem = scratch[34:]
    n = n_gx * n_gy
    gx, gy = lax.axis_index("gx"), lax.axis_index("gy")
    me = gx * n_gy + gy
    own_x, own_y = pl.ds(XO, X), pl.ds(RO, Y)

    loads = (
        pltpu.make_async_copy(u_in, U.at[:, own_x, own_y], loc_sem.at[0]),
        pltpu.make_async_copy(d_in, D.at[0, own_x, own_y], loc_sem.at[1]),
        pltpu.make_async_copy(f_in, F, loc_sem.at[2]),
        pltpu.make_async_copy(hist_in, HI, loc_sem.at[3]),
        pltpu.make_async_copy(crack_in, CR, loc_sem.at[4]),
    )
    for item in loads:
        item.start()

    def peer(i):
        t = lax.rem(me + i, n)
        return (t // n_gy, lax.rem(t, n_gy))

    barrier = pltpu.get_barrier_semaphore()

    def greet(i, c):
        pl.semaphore_signal(barrier, inc=1, device_id=peer(i), device_id_type=MESH)
        return c

    lax.fori_loop(1, n, greet, 0)

    def exists(dx, dy):
        ok = None
        for pos, size, d in ((gx, n_gx, dx), (gy, n_gy, dy)):
            if d:
                one = (pos + d < size) if d > 0 else (pos + d >= 0)
                ok = one if ok is None else jnp.logical_and(ok, one)
        return ok

    def copy_of(number, buf, k):
        comps, xb, xf, rb, rf = WIDTHS[number]
        send_b, send_f, got_b, got_f = stages[4 * number : 4 * number + 4]
        dx, dy = DIRS[k]
        sx = {1: pl.ds(XO + X - xb, xb), -1: pl.ds(XO, xf), 0: own_x}[dx]
        tx = {1: pl.ds(XO - xb, xb), -1: pl.ds(XO + X, xf), 0: own_x}[dx]
        if dy == 0:
            src, dst = buf.at[:, sx, own_y], buf.at[:, tx, own_y]
        elif dy > 0:
            src, dst = send_b.at[:, sx], got_b.at[:, tx]
        else:
            src, dst = send_f.at[:, sx], got_f.at[:, tx]
        return pltpu.make_async_remote_copy(
            src_ref=src,
            dst_ref=dst,
            send_sem=send_sem.at[number, k],
            recv_sem=recv_sem.at[number, k],
            device_id=(gx + dx, gy + dy),
            device_id_type=MESH,
        )

    def send(number, buf):
        comps, xb, xf, rb, rf = WIDTHS[number]
        send_b, send_f = stages[4 * number : 4 * number + 2]

        def go(k):
            pl.when(exists(*DIRS[k]))(lambda: copy_of(number, buf, k).start())

        go(0)
        go(1)

        def pack(x, c):
            for comp in range(comps):
                send_b[comp, x] = buf[comp, x, RO + Y - rb : RO + Y, :]
                send_f[comp, x] = buf[comp, x, RO : RO + rf, :]
            return c

        lax.fori_loop(XO, XO + X, pack, 0, unroll=2)
        for k in range(2, 8):
            go(k)

    def receive(number, buf):
        comps, xb, xf, rb, rf = WIDTHS[number]
        got_b, got_f = stages[4 * number + 2 : 4 * number + 4]
        for k in range(8):
            dx, dy = DIRS[k]
            pl.when(exists(-dx, -dy))(lambda k=k: copy_of(number, buf, k).wait_recv())
        has_b, has_f = gy > 0, gy + 1 < n_gy

        def unpack(x, c):
            for comp in range(comps):
                buf[comp, x, RO - rb : RO, :] = jnp.where(has_b, got_b[comp, x], 0.0)
                buf[comp, x, RO + Y : RO + Y + rf, :] = jnp.where(has_f, got_f[comp, x], 0.0)
            return c

        lax.fori_loop(XO - xb, XO + X + xf, unpack, 0)
        rows = buf.shape[2]

        @pl.when(gx == 0)
        def _():
            buf[:, XO - xb : XO] = jnp.zeros((comps, xb, rows, Z), jnp.float32)

        @pl.when(gx == n_gx - 1)
        def _():
            buf[:, XO + X : XO + X + xf] = jnp.zeros((comps, xf, rows, Z), jnp.float32)

    def sent(number, buf):
        for k in range(8):
            pl.when(exists(*DIRS[k]))(lambda k=k: copy_of(number, buf, k).wait_send())

    def lanes(rows):
        return lax.broadcasted_iota(jnp.int32, (rows, Z), 1)

    def next_z(a):
        return jnp.where(lanes(a.shape[0]) == Z - 1, 0.0, pltpu.roll(a, Z - 1, 1))

    def last_z(a):
        return jnp.where(lanes(a.shape[0]) == 0, 0.0, pltpu.roll(a, 1, 1))

    def inside(x, r0, rows):
        at = lax.broadcasted_iota(jnp.int32, (rows, Z), 0) + (gy * Y + (r0 - RO))
        xg = gx * X + (x - XO)
        top = jnp.where(jnp.logical_and(xg >= 0, xg < n_gx * X), n_gy * Y, 0)
        return jnp.logical_and(at >= 0, at < top)

    def grads(src, x, r0, rows):
        here = [src[c, x, r0 : r0 + rows, :] for c in range(3)]
        result = []
        for c in range(3):
            result.append(
                (
                    src[c, x + 1, r0 : r0 + rows, :] - here[c],
                    src[c, x, r0 + 1 : r0 + 1 + rows, :] - here[c],
                    next_z(here[c]) - here[c],
                )
            )
        return here, result

    def stress(src, x, r0, rows):
        here, d = grads(src, x, r0, rows)
        g = G[x, r0 : r0 + rows, :]
        g2 = g + g
        lam = (1.5 * g) * (d[0][0] + d[1][1] + d[2][2])
        S[0, x, r0 : r0 + rows, :] = g2 * d[0][0] + lam
        S[1, x, r0 : r0 + rows, :] = g2 * d[1][1] + lam
        S[2, x, r0 : r0 + rows, :] = g2 * d[2][2] + lam
        S[3, x, r0 : r0 + rows, :] = g * (d[0][1] + d[1][0])
        S[4, x, r0 : r0 + rows, :] = g * (d[0][2] + d[2][0])
        S[5, x, r0 : r0 + rows, :] = g * (d[1][2] + d[2][1])

    index = ((0, 3, 4), (3, 1, 5), (4, 5, 2))

    def divergence(src, x, r0, rows):
        at = [S[k, x, r0 : r0 + rows, :] for k in range(6)]
        images = []
        for c in range(3):
            ix, iy, iz = index[c]
            total = 0.5 * src[c, x, r0 : r0 + rows, :]
            total = total + (S[ix, x - 1, r0 : r0 + rows, :] - at[ix])
            total = total + (S[iy, x, r0 - 1 : r0 - 1 + rows, :] - at[iy])
            total = total + (last_z(at[iz]) - at[iz])
            images.append(total)
        return images

    def apply_elastic(src, dst, x0, x1, r0, rows, s_rows):
        stress(src, x0 - 1, r0 - 1, s_rows)

        def step(x, c):
            stress(src, x, r0 - 1, s_rows)
            images = divergence(src, x, r0, rows)
            if dst is V0:
                for comp in range(3):
                    V0[comp, x, r0 : r0 + rows, :] = F[comp, x - XO] - images[comp]
            else:
                ok = inside(x, r0, rows)
                for comp in range(3):
                    dst[comp, x, r0 : r0 + rows, :] = jnp.where(ok, images[comp], 0.0)
            return c

        lax.fori_loop(x0, x1, step, 0)

    def fold(a):
        total = a[0:8]
        for k in range(1, a.shape[0] // 8):
            total = total + a[8 * k : 8 * k + 8]
        return total

    def all_sum(number, accs):
        lane = lax.broadcasted_iota(jnp.int32, (1, Z), 1)
        row = jnp.zeros((1, Z), jnp.float32)
        for k, a in enumerate(accs):
            one = jnp.sum(jnp.sum(a, axis=0, keepdims=True), axis=1, keepdims=True)
            row = jnp.where(lane == k, one, row)
        part[number, 0] = row
        gath[number, me] = row

        def go(i, c):
            pltpu.make_async_remote_copy(
                src_ref=part.at[number, 0],
                dst_ref=gath.at[number, me],
                send_sem=ar_send.at[number],
                recv_sem=ar_recv.at[number],
                device_id=peer(i),
                device_id_type=MESH,
            ).start()
            return c

        lax.fori_loop(1, n, go, 0)

    def all_wait(number):
        whole = gath.at[number, pl.ds(0, n - 1)]
        pltpu.make_async_copy(whole, whole, ar_recv.at[number]).wait()
        pltpu.make_async_copy(whole, whole, ar_send.at[number]).wait()
        row = jnp.sum(gath[number], axis=0)
        wide = jnp.broadcast_to(row, (8, Z))
        diag = lax.broadcasted_iota(jnp.int32, (8, Z), 0) == lanes(8)
        column = jnp.sum(jnp.where(diag, wide, 0.0), axis=1, keepdims=True)
        return galerkin(jnp.broadcast_to(column, (8, Z)))

    loads[0].wait()
    loads[1].wait()
    pl.semaphore_wait(barrier, n - 1)
    send(U_EX, U)
    send(D_EX, D)
    receive(D_EX, D)
    all_rows = RO + Y + RO

    def make_gain(x, c):
        left = 1.0 - D[0, x]
        G[x] = jnp.where(inside(x, 0, all_rows), left * left + 0.001, 0.0)
        return c

    lax.fori_loop(XO - 2, XO + X + 2, make_gain, 0)
    loads[2].wait()
    receive(U_EX, U)
    apply_elastic(U, V0, XO, XO + X, RO, Y, Y + 8)
    send(R_EX, V0)
    loads[3].wait()
    loads[4].wait()
    receive(R_EX, V0)
    apply_elastic(V0, V1, XO - 1, XO + X + 2, RO - 1, Y + 8, Y + 8)
    apply_elastic(V1, V2, XO, XO + X + 1, RO - 1, Y + 8, Y + 8)

    def moments(x, accs):
        here, d = grads(V2, x, RO, Y)
        g = G[x, RO : RO + Y, :]
        tr = d[0][0] + d[1][1] + d[2][2]
        s01, s02, s12 = d[0][1] + d[1][0], d[0][2] + d[2][0], d[1][2] + d[2][1]
        normal = d[0][0] * d[0][0] + d[1][1] * d[1][1] + d[2][2] * d[2][2]
        energy = g * (2.0 * normal + (s01 * s01 + s02 * s02 + s12 * s12) + 1.5 * tr * tr)
        v0 = [V0[c, x, RO : RO + Y, :] for c in range(3)]
        v1 = [V1[c, x, RO : RO + Y, :] for c in range(3)]

        def dot(a, b):
            return a[0] * b[0] + a[1] * b[1] + a[2] * b[2]

        m4 = dot(here, here)
        terms = (dot(v0, v0), dot(v0, v1), dot(v1, v1), dot(v1, here), m4, energy + 0.5 * m4)
        return tuple(acc + fold(term) for acc, term in zip(accs, terms))

    zero = tuple(jnp.zeros((8, Z), jnp.float32) for _ in range(6))
    all_sum(0, lax.fori_loop(XO, XO + X, moments, zero))
    sent(U_EX, U)
    sent(R_EX, V0)
    sent(D_EX, D)
    y0, y1, y2 = all_wait(0)

    def move(x, c):
        for comp in range(3):
            rows = pl.ds(RO, Y + 8)
            U[comp, x, rows, :] = (
                U[comp, x, rows, :]
                + y0 * V0[comp, x, rows, :]
                + y1 * V1[comp, x, rows, :]
                + y2 * V2[comp, x, rows, :]
            )
        return c

    lax.fori_loop(XO, XO + X + 1, move, 0)
    u_store = pltpu.make_async_copy(U.at[:, own_x, own_y], u_out, loc_sem.at[5])
    u_store.start()

    def beside(src, x, r0, rows):
        here = src[0, x, r0 : r0 + rows, :]
        ahead = src[0, x + 1, r0 : r0 + rows, :] + src[0, x, r0 + 1 : r0 + 1 + rows, :] + next_z(here)
        behind = src[0, x - 1, r0 : r0 + rows, :] + src[0, x, r0 - 1 : r0 - 1 + rows, :] + last_z(here)
        return here, ahead, behind

    def drive(x, c):
        here, d = grads(U, x, RO, Y)
        tr = d[0][0] + d[1][1] + d[2][2]
        s01, s02, s12 = d[0][1] + d[1][0], d[0][2] + d[2][0], d[1][2] + d[2][1]
        squares = d[0][0] * d[0][0] + d[1][1] * d[1][1] + d[2][2] * d[2][2]
        squares = squares + 0.5 * (s01 * s01 + s02 * s02 + s12 * s12)
        up = jnp.maximum(tr, 0.0)
        psi = (0.5 * (1.5 + 2.0 / 3.0)) * up * up + (squares - tr * tr * (1.0 / 3.0))
        flags = 4.0 * CR[x - XO].astype(jnp.float32)
        h = jnp.maximum(jnp.maximum(HI[x - XO], psi), flags)
        H[0, x, RO : RO + Y, :] = h
        now, ahead, behind = beside(D, x, RO, Y)
        image = (0.5 + 2.0 * h) * now + 2.0 * (6.0 * now - (ahead + behind))
        W0[0, x, RO : RO + Y, :] = 2.0 * h - image
        return c

    lax.fori_loop(XO, XO + X, drive, 0)
    send(W_EX, W0)
    send(H_EX, H)
    h_store = pltpu.make_async_copy(H.at[0, own_x, own_y], h_out, loc_sem.at[6])
    h_store.start()
    receive(W_EX, W0)
    receive(H_EX, H)

    def apply_damage(src, dst, x0, x1):
        r0, rows = RO - 1, Y + 8

        def step(x, c):
            here, ahead, behind = beside(src, x, r0, rows)
            h = H[0, x, r0 : r0 + rows, :]
            image = (0.5 + 2.0 * h) * here + 2.0 * (6.0 * here - (ahead + behind))
            dst[0, x, r0 : r0 + rows, :] = jnp.where(inside(x, r0, rows), image, 0.0)
            return c

        lax.fori_loop(x0, x1, step, 0)

    apply_damage(W0, W1, XO - 1, XO + X + 2)
    apply_damage(W1, W2, XO, XO + X + 1)

    def damage_moments(x, accs):
        w2 = W2[0, x, RO : RO + Y, :]
        ahead = W2[0, x + 1, RO : RO + Y, :] + W2[0, x, RO + 1 : RO + 1 + Y, :] + next_z(w2)
        w0, w1 = W0[0, x, RO : RO + Y, :], W1[0, x, RO : RO + Y, :]
        m5 = w2 * ((12.5 + 2.0 * H[0, x, RO : RO + Y, :]) * w2 - 4.0 * ahead)
        terms = (w0 * w0, w0 * w1, w1 * w1, w1 * w2, w2 * w2, m5)
        return tuple(acc + fold(term) for acc, term in zip(accs, terms))

    all_sum(1, lax.fori_loop(XO, XO + X, damage_moments, zero))
    sent(W_EX, W0)
    sent(H_EX, H)
    y0, y1, y2 = all_wait(1)

    def heal(x, c):
        rows = pl.ds(RO, Y)
        D[0, x, rows, :] = (
            D[0, x, rows, :]
            + y0 * W0[0, x, rows, :]
            + y1 * W1[0, x, rows, :]
            + y2 * W2[0, x, rows, :]
        )
        return c

    lax.fori_loop(XO, XO + X, heal, 0)
    d_store = pltpu.make_async_copy(D.at[0, own_x, own_y], d_out, loc_sem.at[7])
    d_store.start()
    u_store.wait()
    h_store.wait()
    d_store.wait()


def body(n_gx, n_gy, displacement, force, damage, history, crack_flags):
    _, X, Y, Z = displacement.shape
    slabs, rows = XO + X + XF, RO + Y + RO
    n = n_gx * n_gy
    f32 = jnp.float32

    def field(comps):
        return pltpu.VMEM((comps, slabs, rows, Z), f32)

    scratch = [field(3)] * 4 + [field(6), pltpu.VMEM((slabs, rows, Z), f32)]
    scratch += [field(1)] * 5
    scratch += [
        pltpu.VMEM((3, X, Y, Z), f32),
        pltpu.VMEM((X, Y, Z), f32),
        pltpu.VMEM((X, Y, Z), crack_flags.dtype),
    ]
    for number in range(5):
        comps, xb, xf, rb, rf = WIDTHS[number]
        scratch += [pltpu.VMEM((comps, slabs, r, Z), f32) for r in (rb, rf, rb, rf)]
    scratch += [
        pltpu.VMEM((2, 1, 1, Z), f32),
        pltpu.VMEM((2, n, 1, Z), f32),
        pltpu.SemaphoreType.DMA((5, 8)),
        pltpu.SemaphoreType.DMA((5, 8)),
        pltpu.SemaphoreType.DMA((2,)),
        pltpu.SemaphoreType.DMA((2,)),
        pltpu.SemaphoreType.DMA((8,)),
    ]
    scalar = jax.ShapeDtypeStruct((X, Y, Z), f32)
    return pl.pallas_call(
        functools.partial(kernel, (n_gx, n_gy, X, Y, Z)),
        out_shape=(jax.ShapeDtypeStruct(displacement.shape, f32), scalar, scalar),
        in_specs=[pl.BlockSpec(memory_space=pl.ANY)] * 5,
        out_specs=tuple([pl.BlockSpec(memory_space=pl.ANY)] * 3),
        scratch_shapes=scratch,
        compiler_params=pltpu.CompilerParams(
            collective_id=0, has_side_effects=True, vmem_limit_bytes=48 * 1024 * 1024
        ),
    )(displacement, force, damage, history, crack_flags)


def solution(mesh):
    return jax.shard_map(
        functools.partial(body, mesh.shape["gx"], mesh.shape["gy"]),
        mesh=mesh,
        in_specs=(
            P(None, "gx", "gy", None),
            P(None, "gx", "gy", None),
            P("gx", "gy", None),
            P("gx", "gy", None),
            P("gx", "gy", None),
        ),
        out_specs=(P(None, "gx", "gy", None), P("gx", "gy", None), P("gx", "gy", None)),
        check_vma=False,
    )
```

time: 440 us -> 56.2 us (0.13)
  blocking collectives: 248 us -> 0 us
  starting transfers between devices: 71.3 us -> 0 us
  waiting for transfers between devices: 62.3 us -> 0 us
  Pallas kernels: 0 us -> 47.9 us
  other arithmetic: 33.1 us -> 0 us
  between operations: 20.7 us -> 0.65 us
  local copies, waits for them, and re-layouts: 2.15 us -> 7.39 us
    psum x6 -> x0, blocking collectives: 248 us -> none  [paired_sums(): lax.psum((jnp.sum(resid * resid), jnp.sum(resid * image)), ('gx', 'gy'))]
    ppermute x36 -> x0, starting transfers between devices: 71.3 us -> none  [the longest x18 47.6 us: padded_2(): before = lax.ppermute(last, axis, up)]
    ppermute x36 -> x0, waiting for transfers between devices: 62.3 us -> none  [the longest x18 61.3 us: padded_2(): after = lax.ppermute(leading, axis, down)]
    pallas_call x0 -> x1, Pallas kernels: none -> 47.9 us  [body(): pl.pallas_call(functools.partial(kernel, (n_gx, n_gy, X, Y, Z)), out_shap...]
    mul x8 -> x0, other arithmetic: 7.79 us -> none  [the longest x4 4.65 us: elastic(): weight * (2.0 * shear_modulus * strain[index])]
    unnamed x28 -> x13, local copies, waits for them, and re-layouts: 1.17 us -> 7.39 us
    reduce_sum x6 -> x0, other arithmetic: 6.07 us -> none  [paired_sums(): jnp.sum(resid * image)]
    another operation x9 -> x0, other arithmetic: 5.8 us -> none  [the longest x8 4.73 us: elastic(): return (jnp.stack(images), strain)]
  transfers between devices with their start and end apart: 36 -> 0, of which waited for: 21 -> 0; matrix products, arithmetic and copies ran while one was open for 0% -> 0% of each run, Pallas kernels for 0% -> 0%
where the time goes in v1:
time: 56.2 us; the launch traced here: 55.9 us
  Pallas kernels  47.9 us (85%)
  local copies, waits for them, and re-layouts  7.39 us (13%)
  between operations  0.65 us (1%)
    pallas_call x1, Pallas kernels, body(): pl.pallas_call(functools.partial(kernel, (n_gx, n_gy, X, Y, Z)), out_shap...  47.9 us
    unnamed x13, local copies, waits for them, and re-layouts  7.39 us

profile of v1, /device:TPU:0, one launch (start us, length us, event | category | flops | bytes accessed | tf_op | source)
XLA Modules:
  0.0 55.9 jit_solution(12368286227255240566)
XLA Ops:
  0.6 0.0 copy-start
  0.6 1.1 %copy-done = f32[3,16,32,128]{3,2,1,0:T(8,128)S(1)} copy-done((f32[3,16,32,128]{3,2,1,0:T(8,128)S(1)}, f32[3,16,32,128]{3,2,1,0:T(8,128)}, u32[]{:S(2)}) %copy-start) | copy-done | bytes 786456
  1.8 0.0 copy-start.1
  1.8 1.1 %copy-done.1 = f32[3,16,32,128]{3,2,1,0:T(8,128)S(1)} copy-done((f32[3,16,32,128]{3,2,1,0:T(8,128)S(1)}, f32[3,16,32,128]{3,2,1,0:T(8,128)}, u32[]{:S(2)}) %copy-start.1) | copy-done | bytes 786456
  2.9 0.0 copy-start.2
  2.9 0.9 %copy-done.2 = f32[16,32,128]{2,1,0:T(8,128)S(1)} copy-done((f32[16,32,128]{2,1,0:T(8,128)S(1)}, f32[16,32,128]{2,1,0:T(8,128)}, u32[]{:S(2)}) %copy-start.2) | copy-done | bytes 262168
  3.9 0.0 copy-start.3
  3.9 0.9 %copy-done.3 = f32[16,32,128]{2,1,0:T(8,128)S(1)} copy-done((f32[16,32,128]{2,1,0:T(8,128)S(1)}, f32[16,32,128]{2,1,0:T(8,128)}, u32[]{:S(2)}) %copy-start.3) | copy-done | bytes 262168
  4.8 0.0 copy-start.4
  4.8 0.9 %copy-done.4 = s32[16,32,128]{2,1,0:T(8,128)S(1)} copy-done((s32[16,32,128]{2,1,0:T(8,128)S(1)}, s32[16,32,128]{2,1,0:T(8,128)}, u32[]{:S(2)}) %copy-start.4) | copy-done | bytes 262168
  5.8 47.9 %shard_map.76 = (f32[3,16,32,128]{3,2,1,0:T(8,128)S(1)}, f32[16,32,128]{2,1,0:T(8,128)S(1)}, f32[16,32,128]{2,1,0:T(8,128)S(1)}) custom-call(f32[3,16,32,128]{3,2,1,0:T(8,128)S(1)} %copy-done, f32[3,16,32,128]{3,2,1,0:T(8,128)S(1)} %copy-done.1, f32[16,32,128]{2,1,0:T(8,128)S(1)} %copy-done.2, f32[16,32,128]{2,1,0:T(8,128)S(1)} %copy-done.3, ...), custom_call_target="tpu_custom_call" | custom-call | tf_op jit(solution)/shard_map/pallas_call | solution.py:428
  53.6 0.9 %copy.11 = f32[3,16,32,128]{3,2,1,0:T(8,128)} copy(f32[3,16,32,128]{3,2,1,0:T(8,128)S(1)} %get-tuple-element.6) | data formatting | bytes 1572864
  54.5 0.7 %copy.12 = f32[16,32,128]{2,1,0:T(8,128)} copy(f32[16,32,128]{2,1,0:T(8,128)S(1)} %get-tuple-element.7) | data formatting | bytes 524288
  55.2 0.7 %copy.13 = f32[16,32,128]{2,1,0:T(8,128)} copy(f32[16,32,128]{2,1,0:T(8,128)S(1)} %get-tuple-element.8) | data formatting | bytes 524288
Async XLA Ops:
  0.6 1.1 %copy-start = (f32[3,16,32,128]{3,2,1,0:T(8,128)S(1)}, f32[3,16,32,128]{3,2,1,0:T(8,128)}, u32[]{:S(2)}) copy-start(f32[3,16,32,128]{3,2,1,0:T(8,128)} %u_in.1) | copy-start | bytes 2359300
  1.8 1.1 %copy-start.1 = (f32[3,16,32,128]{3,2,1,0:T(8,128)S(1)}, f32[3,16,32,128]{3,2,1,0:T(8,128)}, u32[]{:S(2)}) copy-start(f32[3,16,32,128]{3,2,1,0:T(8,128)} %f_in.1) | copy-start | bytes 2359300
  2.9 0.9 %copy-start.2 = (f32[16,32,128]{2,1,0:T(8,128)S(1)}, f32[16,32,128]{2,1,0:T(8,128)}, u32[]{:S(2)}) copy-start(f32[16,32,128]{2,1,0:T(8,128)} %d_in.1) | copy-start | bytes 786436
  3.9 0.9 %copy-start.3 = (f32[16,32,128]{2,1,0:T(8,128)S(1)}, f32[16,32,128]{2,1,0:T(8,128)}, u32[]{:S(2)}) copy-start(f32[16,32,128]{2,1,0:T(8,128)} %hist_in.1) | copy-start | bytes 786436
  4.8 0.9 %copy-start.4 = (s32[16,32,128]{2,1,0:T(8,128)S(1)}, s32[16,32,128]{2,1,0:T(8,128)}, u32[]{:S(2)}) copy-start(s32[16,32,128]{2,1,0:T(8,128)} %crack_in.1) | copy-start | bytes 786436

commit v2 on v1

--- a/solution.py
+++ b/solution.py
@@ -6,6 +6,9 @@
 from jax.experimental.pallas import tpu as pltpu
 from jax.sharding import PartitionSpec as P
 
+UNROLL = 4
+SHIFT_U = 8.0
+SHIFT_D = 15.0
 XO = 2
 XF = 3
 RO = 8
@@ -21,20 +24,22 @@
 }
 
 
-def galerkin(total):
-    m = [total[k : k + 1, :] for k in range(6)]
-    l10, l20 = m[2] / m[1], m[3] / m[1]
-    d1 = m[3] - l10 * m[2]
-    e1 = m[4] - l20 * m[2]
+def galerkin(total, shift):
+    g00, g01, g02, g11, g12, g22, h22 = [total[k : k + 1, :] for k in range(7)]
+    h00, h01, h02 = g01 + shift * g00, g11 + shift * g01, g12 + shift * g02
+    h11, h12 = g12 + shift * g11, g22 + shift * g12
+    l10, l20 = h01 / h00, h02 / h00
+    d1 = h11 - l10 * h01
+    e1 = h12 - l20 * h01
     l21 = e1 / d1
-    f1 = m[5] - l20 * m[3] - l21 * e1
-    z1 = m[1] - l10 * m[0]
-    z2 = m[2] - l20 * m[0] - l21 * z1
+    f1 = h22 - l20 * h02 - l21 * e1
+    z1 = g01 - l10 * g00
+    z2 = g02 - l20 * g00 - l21 * z1
     y2 = jnp.where(f1 > 0.0, z2 / f1, 0.0)
     y1 = jnp.where(d1 > 0.0, z1 / d1 - l21 * y2, 0.0)
     y2 = jnp.where(d1 > 0.0, y2, 0.0)
-    y0 = m[0] / m[1] - l10 * y1 - l20 * y2
-    y0 = jnp.where(d1 > 0.0, y0, m[0] / m[1])
+    y0 = g00 / h00 - l10 * y1 - l20 * y2
+    y0 = jnp.where(d1 > 0.0, y0, g00 / h00)
     return y0, y1, y2
 
 
@@ -115,7 +120,7 @@
                 send_f[comp, x] = buf[comp, x, RO : RO + rf, :]
             return c
 
-        lax.fori_loop(XO, XO + X, pack, 0, unroll=2)
+        lax.fori_loop(XO, XO + X, pack, 0, unroll=UNROLL)
         for k in range(2, 8):
             go(k)
 
@@ -133,7 +138,7 @@
                 buf[comp, x, RO + Y : RO + Y + rf, :] = jnp.where(has_f, got_f[comp, x], 0.0)
             return c
 
-        lax.fori_loop(XO - xb, XO + X + xf, unpack, 0)
+        lax.fori_loop(XO - xb, XO + X + xf, unpack, 0, unroll=UNROLL)
         rows = buf.shape[2]
 
         @pl.when(gx == 0)
@@ -190,12 +195,12 @@
 
     index = ((0, 3, 4), (3, 1, 5), (4, 5, 2))
 
-    def divergence(src, x, r0, rows):
+    def divergence(src, x, r0, rows, spring):
         at = [S[k, x, r0 : r0 + rows, :] for k in range(6)]
         images = []
         for c in range(3):
             ix, iy, iz = index[c]
-            total = 0.5 * src[c, x, r0 : r0 + rows, :]
+            total = spring * src[c, x, r0 : r0 + rows, :]
             total = total + (S[ix, x - 1, r0 : r0 + rows, :] - at[ix])
             total = total + (S[iy, x, r0 - 1 : r0 - 1 + rows, :] - at[iy])
             total = total + (last_z(at[iz]) - at[iz])
@@ -203,11 +208,16 @@
         return images
 
     def apply_elastic(src, dst, x0, x1, r0, rows, s_rows):
-        stress(src, x0 - 1, r0 - 1, s_rows)
+        spring = 0.5 if dst is V0 else 0.5 - SHIFT_U
+
+        def strain_step(x, c):
+            stress(src, x, r0 - 1, s_rows)
+            return c
+
+        lax.fori_loop(x0 - 1, x1, strain_step, 0, unroll=UNROLL)
 
         def step(x, c):
-            stress(src, x, r0 - 1, s_rows)
-            images = divergence(src, x, r0, rows)
+            images = divergence(src, x, r0, rows, spring)
             if dst is V0:
                 for comp in range(3):
                     V0[comp, x, r0 : r0 + rows, :] = F[comp, x - XO] - images[comp]
@@ -217,7 +227,7 @@
                     dst[comp, x, r0 : r0 + rows, :] = jnp.where(ok, images[comp], 0.0)
             return c
 
-        lax.fori_loop(x0, x1, step, 0)
+        lax.fori_loop(x0, x1, step, 0, unroll=UNROLL)
 
     def fold(a):
         total = a[0:8]
@@ -247,7 +257,7 @@
 
         lax.fori_loop(1, n, go, 0)
 
-    def all_wait(number):
+    def all_wait(number, shift):
         whole = gath.at[number, pl.ds(0, n - 1)]
         pltpu.make_async_copy(whole, whole, ar_recv.at[number]).wait()
         pltpu.make_async_copy(whole, whole, ar_send.at[number]).wait()
@@ -255,7 +265,7 @@
         wide = jnp.broadcast_to(row, (8, Z))
         diag = lax.broadcasted_iota(jnp.int32, (8, Z), 0) == lanes(8)
         column = jnp.sum(jnp.where(diag, wide, 0.0), axis=1, keepdims=True)
-        return galerkin(jnp.broadcast_to(column, (8, Z)))
+        return galerkin(jnp.broadcast_to(column, (8, Z)), shift)
 
     loads[0].wait()
     loads[1].wait()
@@ -270,7 +280,7 @@
         G[x] = jnp.where(inside(x, 0, all_rows), left * left + 0.001, 0.0)
         return c
 
-    lax.fori_loop(XO - 2, XO + X + 2, make_gain, 0)
+    lax.fori_loop(XO - 2, XO + X + 2, make_gain, 0, unroll=UNROLL)
     loads[2].wait()
     receive(U_EX, U)
     apply_elastic(U, V0, XO, XO + X, RO, Y, Y + 8)
@@ -295,15 +305,16 @@
             return a[0] * b[0] + a[1] * b[1] + a[2] * b[2]
 
         m4 = dot(here, here)
-        terms = (dot(v0, v0), dot(v0, v1), dot(v1, v1), dot(v1, here), m4, energy + 0.5 * m4)
+        terms = (dot(v0, v0), dot(v0, v1), dot(v0, here), dot(v1, v1))
+        terms = terms + (dot(v1, here), m4, energy + 0.5 * m4)
         return tuple(acc + fold(term) for acc, term in zip(accs, terms))
 
-    zero = tuple(jnp.zeros((8, Z), jnp.float32) for _ in range(6))
-    all_sum(0, lax.fori_loop(XO, XO + X, moments, zero))
+    zero = tuple(jnp.zeros((8, Z), jnp.float32) for _ in range(7))
+    all_sum(0, lax.fori_loop(XO, XO + X, moments, zero, unroll=2))
     sent(U_EX, U)
     sent(R_EX, V0)
     sent(D_EX, D)
-    y0, y1, y2 = all_wait(0)
+    y0, y1, y2 = all_wait(0, SHIFT_U)
 
     def move(x, c):
         for comp in range(3):
@@ -316,7 +327,7 @@
             )
         return c
 
-    lax.fori_loop(XO, XO + X + 1, move, 0)
+    lax.fori_loop(XO, XO + X + 1, move, 0, unroll=2)
     u_store = pltpu.make_async_copy(U.at[:, own_x, own_y], u_out, loc_sem.at[5])
     u_store.start()
 
@@ -342,7 +353,7 @@
         W0[0, x, RO : RO + Y, :] = 2.0 * h - image
         return c
 
-    lax.fori_loop(XO, XO + X, drive, 0)
+    lax.fori_loop(XO, XO + X, drive, 0, unroll=2)
     send(W_EX, W0)
     send(H_EX, H)
     h_store = pltpu.make_async_copy(H.at[0, own_x, own_y], h_out, loc_sem.at[6])
@@ -356,11 +367,11 @@
         def step(x, c):
             here, ahead, behind = beside(src, x, r0, rows)
             h = H[0, x, r0 : r0 + rows, :]
-            image = (0.5 + 2.0 * h) * here + 2.0 * (6.0 * here - (ahead + behind))
+            image = ((12.5 - SHIFT_D) + 2.0 * h) * here - 2.0 * (ahead + behind)
             dst[0, x, r0 : r0 + rows, :] = jnp.where(inside(x, r0, rows), image, 0.0)
             return c
 
-        lax.fori_loop(x0, x1, step, 0)
+        lax.fori_loop(x0, x1, step, 0, unroll=UNROLL)
 
     apply_damage(W0, W1, XO - 1, XO + X + 2)
     apply_damage(W1, W2, XO, XO + X + 1)
@@ -370,13 +381,13 @@
         ahead = W2[0, x + 1, RO : RO + Y, :] + W2[0, x, RO + 1 : RO + 1 + Y, :] + next_z(w2)
         w0, w1 = W0[0, x, RO : RO + Y, :], W1[0, x, RO : RO + Y, :]
         m5 = w2 * ((12.5 + 2.0 * H[0, x, RO : RO + Y, :]) * w2 - 4.0 * ahead)
-        terms = (w0 * w0, w0 * w1, w1 * w1, w1 * w2, w2 * w2, m5)
+        terms = (w0 * w0, w0 * w1, w0 * w2, w1 * w1, w1 * w2, w2 * w2, m5)
         return tuple(acc + fold(term) for acc, term in zip(accs, terms))
 
-    all_sum(1, lax.fori_loop(XO, XO + X, damage_moments, zero))
+    all_sum(1, lax.fori_loop(XO, XO + X, damage_moments, zero, unroll=2))
     sent(W_EX, W0)
     sent(H_EX, H)
-    y0, y1, y2 = all_wait(1)
+    y0, y1, y2 = all_wait(1, SHIFT_D)
 
     def heal(x, c):
         rows = pl.ds(RO, Y)
@@ -388,7 +399,7 @@
         )
         return c
 
-    lax.fori_loop(XO, XO + X, heal, 0)
+    lax.fori_loop(XO, XO + X, heal, 0, unroll=UNROLL)
     d_store = pltpu.make_async_copy(D.at[0, own_x, own_y], d_out, loc_sem.at[7])
     d_store.start()
     u_store.wait()
@@ -428,11 +439,11 @@
     return pl.pallas_call(
         functools.partial(kernel, (n_gx, n_gy, X, Y, Z)),
         out_shape=(jax.ShapeDtypeStruct(displacement.shape, f32), scalar, scalar),
-        in_specs=[pl.BlockSpec(memory_space=pl.ANY)] * 5,
+        in_specs=[pl.BlockSpec(memory_space=pltpu.HBM)] * 5,
         out_specs=tuple([pl.BlockSpec(memory_space=pl.ANY)] * 3),
         scratch_shapes=scratch,
         compiler_params=pltpu.CompilerParams(
-            collective_id=0, has_side_effects=True, vmem_limit_bytes=48 * 1024 * 1024
+            collective_id=0, has_side_effects=True, vmem_limit_bytes=67043328
         ),
     )(displacement, force, damage, history, crack_flags)
 

time: 56.2 us -> 43.7 us (0.78)
  Pallas kernels: 47.9 us -> 39 us
  local copies, waits for them, and re-layouts: 7.39 us -> 3.86 us
    pallas_call x1, Pallas kernels: 47.9 us -> 39 us  [body(): pl.pallas_call(functools.partial(kernel, (n_gx, n_gy, X, Y, Z)), out_shap...]
    unnamed x13 -> x7, local copies, waits for them, and re-layouts: 7.39 us -> 3.86 us
where the time goes in v2:
time: 43.7 us; the launch traced here: 43.5 us
  Pallas kernels  39 us (89%)
  local copies, waits for them, and re-layouts  3.86 us (9%)
  between operations  0.65 us (1%)
    pallas_call x1, Pallas kernels, body(): pl.pallas_call(functools.partial(kernel, (n_gx, n_gy, X, Y, Z)), out_shap...  39 us
    unnamed x7, local copies, waits for them, and re-layouts  3.86 us

profile of v2, /device:TPU:0, one launch (start us, length us, event | category | flops | bytes accessed | tf_op | source)
XLA Modules:
  0.0 43.5 jit_solution(11347299887160213240)
XLA Ops:
  0.6 39.0 %shard_map.76 = (f32[3,16,32,128]{3,2,1,0:T(8,128)}, f32[16,32,128]{2,1,0:T(8,128)}, f32[16,32,128]{2,1,0:T(8,128)}) custom-call(f32[3,16,32,128]{3,2,1,0:T(8,128)} %u_in.1, f32[3,16,32,128]{3,2,1,0:T(8,128)} %f_in.1, f32[16,32,128]{2,1,0:T(8,128)} %d_in.1, f32[16,32,128]{2,1,0:T(8,128)} %hist_in.1, s32[16,32,128]{2,1,0:T(8,128)} %crack_in.1), custom_call_target="tpu_custom_call" | custom-call | tf_op jit(solution)/shard_map/pallas_call | solution.py:439
  39.6 0.0 copy-start.1
  39.6 2.1 %copy.11 = f32[3,16,32,128]{3,2,1,0:T(8,128)} copy(f32[3,16,32,128]{3,2,1,0:T(8,128)} %get-tuple-element.6) | data formatting | bytes 1572864
  41.7 0.0 copy-done.1
  41.7 0.0 copy-start
  41.7 0.7 %copy.12 = f32[16,32,128]{2,1,0:T(8,128)} copy(f32[16,32,128]{2,1,0:T(8,128)S(1)} %copy-done.1) | data formatting | bytes 524288
  42.4 0.3 copy-done
  42.8 0.7 %copy.13 = f32[16,32,128]{2,1,0:T(8,128)} copy(f32[16,32,128]{2,1,0:T(8,128)S(1)} %copy-done) | data formatting | bytes 524288
Async XLA Ops:
  39.6 2.1 %copy-start.1 = (f32[16,32,128]{2,1,0:T(8,128)S(1)}, f32[16,32,128]{2,1,0:T(8,128)}, u32[]{:S(2)}) copy-start(f32[16,32,128]{2,1,0:T(8,128)} %get-tuple-element.7) | copy-start | bytes 786436
  41.7 1.0 %copy-start = (f32[16,32,128]{2,1,0:T(8,128)S(1)}, f32[16,32,128]{2,1,0:T(8,128)}, u32[]{:S(2)}) copy-start(f32[16,32,128]{2,1,0:T(8,128)} %get-tuple-element.8) | copy-start | bytes 786436

commit v3 on v2

--- a/solution.py
+++ b/solution.py
@@ -18,10 +18,14 @@
 WIDTHS = {
     U_EX: (3, 1, 1, 1, 1),
     D_EX: (1, 2, 2, 2, 2),
-    R_EX: (3, 2, 3, 2, 4),
-    W_EX: (1, 2, 3, 2, 4),
+    R_EX: (3, 2, 3, 2, 3),
+    W_EX: (1, 2, 3, 2, 3),
     H_EX: (1, 1, 2, 1, 2),
 }
+
+
+def pieces(rows):
+    return [(j, j, 1) for j in range(3)] if rows == 3 else [(0, 0, rows)]
 
 
 def galerkin(total, shift):
@@ -111,17 +115,18 @@
         def go(k):
             pl.when(exists(*DIRS[k]))(lambda: copy_of(number, buf, k).start())
 
-        go(0)
-        go(1)
-
         def pack(x, c):
             for comp in range(comps):
-                send_b[comp, x] = buf[comp, x, RO + Y - rb : RO + Y, :]
-                send_f[comp, x] = buf[comp, x, RO : RO + rf, :]
+                for j, at, w in pieces(rb):
+                    r0 = RO + Y - rb + at
+                    send_b[comp, x, j] = buf[comp, x, r0 : r0 + w, :]
+                for j, at, w in pieces(rf):
+                    r0 = RO + at
+                    send_f[comp, x, j] = buf[comp, x, r0 : r0 + w, :]
             return c
 
         lax.fori_loop(XO, XO + X, pack, 0, unroll=UNROLL)
-        for k in range(2, 8):
+        for k in (4, 5, 6, 7, 2, 3, 0, 1):
             go(k)
 
     def receive(number, buf):
@@ -134,8 +139,12 @@
 
         def unpack(x, c):
             for comp in range(comps):
-                buf[comp, x, RO - rb : RO, :] = jnp.where(has_b, got_b[comp, x], 0.0)
-                buf[comp, x, RO + Y : RO + Y + rf, :] = jnp.where(has_f, got_f[comp, x], 0.0)
+                for j, at, w in pieces(rb):
+                    r0 = RO - rb + at
+                    buf[comp, x, r0 : r0 + w, :] = jnp.where(has_b, got_b[comp, x, j], 0.0)
+                for j, at, w in pieces(rf):
+                    r0 = RO + Y + at
+                    buf[comp, x, r0 : r0 + w, :] = jnp.where(has_f, got_f[comp, x, j], 0.0)
             return c
 
         lax.fori_loop(XO - xb, XO + X + xf, unpack, 0, unroll=UNROLL)
@@ -407,6 +416,15 @@
     d_store.wait()
 
 
+def store_results(u, d, h, u_out, d_out, h_out, sem):
+    pairs = ((u, u_out), (d, d_out), (h, h_out))
+    copies = [pltpu.make_async_copy(a, b, sem.at[k]) for k, (a, b) in enumerate(pairs)]
+    for item in copies:
+        item.start()
+    for item in copies:
+        item.wait()
+
+
 def body(n_gx, n_gy, displacement, force, damage, history, crack_flags):
     _, X, Y, Z = displacement.shape
     slabs, rows = XO + X + XF, RO + Y + RO
@@ -425,7 +443,9 @@
     ]
     for number in range(5):
         comps, xb, xf, rb, rf = WIDTHS[number]
-        scratch += [pltpu.VMEM((comps, slabs, r, Z), f32) for r in (rb, rf, rb, rf)]
+        for r in (rb, rf, rb, rf):
+            parts = pieces(r)
+            scratch.append(pltpu.VMEM((comps, slabs, len(parts), parts[0][2], Z), f32))
     scratch += [
         pltpu.VMEM((2, 1, 1, Z), f32),
         pltpu.VMEM((2, n, 1, Z), f32),
@@ -436,16 +456,24 @@
         pltpu.SemaphoreType.DMA((8,)),
     ]
     scalar = jax.ShapeDtypeStruct((X, Y, Z), f32)
-    return pl.pallas_call(
+    given = (displacement, force, damage, history, crack_flags)
+    results = pl.pallas_call(
         functools.partial(kernel, (n_gx, n_gy, X, Y, Z)),
-        out_shape=(jax.ShapeDtypeStruct(displacement.shape, f32), scalar, scalar),
+        out_shape=tuple(pltpu.VMEM(a.shape, f32) for a in (displacement, damage, history)),
         in_specs=[pl.BlockSpec(memory_space=pltpu.HBM)] * 5,
         out_specs=tuple([pl.BlockSpec(memory_space=pl.ANY)] * 3),
         scratch_shapes=scratch,
         compiler_params=pltpu.CompilerParams(
-            collective_id=0, has_side_effects=True, vmem_limit_bytes=67043328
+            collective_id=0, has_side_effects=True, vmem_limit_bytes=48 * 1024 * 1024
         ),
-    )(displacement, force, damage, history, crack_flags)
+    )(*[pltpu.with_memory_space_constraint(a, pltpu.HBM) for a in given])
+    return pl.pallas_call(
+        store_results,
+        out_shape=(jax.ShapeDtypeStruct(displacement.shape, f32), scalar, scalar),
+        in_specs=[pl.BlockSpec(memory_space=pltpu.VMEM)] * 3,
+        out_specs=tuple([pl.BlockSpec(memory_space=pl.ANY)] * 3),
+        scratch_shapes=[pltpu.SemaphoreType.DMA((3,))],
+    )(*[pltpu.with_memory_space_constraint(a, pltpu.VMEM) for a in results])
 
 
 def solution(mesh):

time: 43.7 us -> 40.1 us (0.918)
  local copies, waits for them, and re-layouts: 3.86 us -> 0 us
    unnamed x7 -> x0, local copies, waits for them, and re-layouts: 3.86 us -> none
    pallas_call x0 -> x1, Pallas kernels: none -> 1.08 us  [body(): pl.pallas_call(store_results, out_shape=(jax.ShapeDtypeStruct(displacemen...]
    pallas_call x1, Pallas kernels: 39 us -> 38.2 us  [body(): pl.pallas_call(functools.partial(kernel, (n_gx, n_gy, X, Y, Z)), out_shap...]
where the time goes in v3:
time: 40.1 us; the launch traced here: 40 us
  Pallas kernels  39.3 us (98%)
  between operations  0.64 us (2%)
    pallas_call x1, Pallas kernels, body(): pl.pallas_call(functools.partial(kernel, (n_gx, n_gy, X, Y, Z)), out_shap...  38.2 us
    pallas_call x1, Pallas kernels, body(): pl.pallas_call(store_results, out_shape=(jax.ShapeDtypeStruct(displacemen...  1.08 us

profile of v3, /device:TPU:0, one launch (start us, length us, event | category | flops | bytes accessed | tf_op | source)
XLA Modules:
  0.0 40.0 jit_solution(9485991596318634232)
XLA Ops:
  0.6 38.2 %shard_map.76 = (f32[3,16,32,128]{3,2,1,0:T(8,128)S(1)}, f32[16,32,128]{2,1,0:T(8,128)S(1)}, f32[16,32,128]{2,1,0:T(8,128)S(1)}) custom-call(f32[3,16,32,128]{3,2,1,0:T(8,128)} %u_in.1, f32[3,16,32,128]{3,2,1,0:T(8,128)} %f_in.1, f32[16,32,128]{2,1,0:T(8,128)} %d_in.1, f32[16,32,128]{2,1,0:T(8,128)} %hist_in.1, s32[16,32,128]{2,1,0:T(8,128)} %crack_in.1), custom_call_target="tpu_custom_call" | custom-call | tf_op jit(solution)/shard_map/pallas_call | solution.py:460
  38.9 1.1 %shard_map.77 = (f32[3,16,32,128]{3,2,1,0:T(8,128)}, f32[16,32,128]{2,1,0:T(8,128)}, f32[16,32,128]{2,1,0:T(8,128)}) custom-call(f32[3,16,32,128]{3,2,1,0:T(8,128)S(1)} %get-tuple-element.6.u, f32[16,32,128]{2,1,0:T(8,128)S(1)} %get-tuple-element.7.d, f32[16,32,128]{2,1,0:T(8,128)S(1)} %get-tuple-element.8.h), custom_call_target="tpu_custom_call" | custom-call | tf_op jit(solution)/shard_map/pallas_call | solution.py:470

commit v4 on v3

--- a/solution.py
+++ b/solution.py
@@ -6,7 +6,7 @@
 from jax.experimental.pallas import tpu as pltpu
 from jax.sharding import PartitionSpec as P
 
-UNROLL = 4
+UNROLL = 8
 SHIFT_U = 8.0
 SHIFT_D = 15.0
 XO = 2
@@ -67,17 +67,28 @@
     for item in loads:
         item.start()
 
-    def peer(i):
-        t = lax.rem(me + i, n)
-        return (t // n_gy, lax.rem(t, n_gy))
+    def each_peer(act):
+        def wrapped(at, size):
+            return jnp.where(at >= size, at - size, at)
+
+        ys = [wrapped(gy + dy, n_gy) for dy in range(n_gy)]
+
+        def column(dx, c):
+            tx = wrapped(gx + dx, n_gx)
+            for ty in ys:
+                act((tx, ty))
+            return c
+
+        for ty in ys[1:]:
+            act((gx, ty))
+        lax.fori_loop(1, n_gx, column, 0)
 
     barrier = pltpu.get_barrier_semaphore()
 
-    def greet(i, c):
-        pl.semaphore_signal(barrier, inc=1, device_id=peer(i), device_id_type=MESH)
-        return c
-
-    lax.fori_loop(1, n, greet, 0)
+    def greet(device):
+        pl.semaphore_signal(barrier, inc=1, device_id=device, device_id_type=MESH)
+
+    each_peer(greet)
 
     def exists(dx, dy):
         ok = None
@@ -125,8 +136,10 @@
                     send_f[comp, x, j] = buf[comp, x, r0 : r0 + w, :]
             return c
 
+        go(0)
+        go(1)
         lax.fori_loop(XO, XO + X, pack, 0, unroll=UNROLL)
-        for k in (4, 5, 6, 7, 2, 3, 0, 1):
+        for k in (4, 5, 6, 7, 2, 3):
             go(k)
 
     def receive(number, buf):
@@ -253,18 +266,17 @@
         part[number, 0] = row
         gath[number, me] = row
 
-        def go(i, c):
+        def go(device):
             pltpu.make_async_remote_copy(
                 src_ref=part.at[number, 0],
                 dst_ref=gath.at[number, me],
                 send_sem=ar_send.at[number],
                 recv_sem=ar_recv.at[number],
-                device_id=peer(i),
+                device_id=device,
                 device_id_type=MESH,
             ).start()
-            return c
-
-        lax.fori_loop(1, n, go, 0)
+
+        each_peer(go)
 
     def all_wait(number, shift):
         whole = gath.at[number, pl.ds(0, n - 1)]
@@ -319,7 +331,7 @@
         return tuple(acc + fold(term) for acc, term in zip(accs, terms))
 
     zero = tuple(jnp.zeros((8, Z), jnp.float32) for _ in range(7))
-    all_sum(0, lax.fori_loop(XO, XO + X, moments, zero, unroll=2))
+    all_sum(0, lax.fori_loop(XO, XO + X, moments, zero, unroll=4))
     sent(U_EX, U)
     sent(R_EX, V0)
     sent(D_EX, D)
@@ -336,7 +348,7 @@
             )
         return c
 
-    lax.fori_loop(XO, XO + X + 1, move, 0, unroll=2)
+    lax.fori_loop(XO, XO + X + 1, move, 0, unroll=4)
     u_store = pltpu.make_async_copy(U.at[:, own_x, own_y], u_out, loc_sem.at[5])
     u_store.start()
 
@@ -362,7 +374,7 @@
         W0[0, x, RO : RO + Y, :] = 2.0 * h - image
         return c
 
-    lax.fori_loop(XO, XO + X, drive, 0, unroll=2)
+    lax.fori_loop(XO, XO + X, drive, 0, unroll=4)
     send(W_EX, W0)
     send(H_EX, H)
     h_store = pltpu.make_async_copy(H.at[0, own_x, own_y], h_out, loc_sem.at[6])
@@ -393,7 +405,7 @@
         terms = (w0 * w0, w0 * w1, w0 * w2, w1 * w1, w1 * w2, w2 * w2, m5)
         return tuple(acc + fold(term) for acc, term in zip(accs, terms))
 
-    all_sum(1, lax.fori_loop(XO, XO + X, damage_moments, zero, unroll=2))
+    all_sum(1, lax.fori_loop(XO, XO + X, damage_moments, zero, unroll=4))
     sent(W_EX, W0)
     sent(H_EX, H)
     y0, y1, y2 = all_wait(1, SHIFT_D)

time: 40.1 us -> 37.7 us (0.940)
  Pallas kernels: 39.3 us -> 36.9 us
    pallas_call x1, Pallas kernels: 38.2 us -> 35.8 us  [body(): pl.pallas_call(functools.partial(kernel, (n_gx, n_gy, X, Y, Z)), out_shap...]
where the time goes in v4:
time: 37.7 us; the launch traced here: 37.5 us
  Pallas kernels  36.9 us (98%)
  between operations  0.64 us (2%)
    pallas_call x1, Pallas kernels, body(): pl.pallas_call(functools.partial(kernel, (n_gx, n_gy, X, Y, Z)), out_shap...  35.8 us
    pallas_call x1, Pallas kernels, body(): pl.pallas_call(store_results, out_shape=(jax.ShapeDtypeStruct(displacemen...  1.08 us

profile of v4, /device:TPU:0, one launch (start us, length us, event | category | flops | bytes accessed | tf_op | source)
XLA Modules:
  0.0 37.5 jit_solution(1709931138147986534)
XLA Ops:
  0.6 35.8 %shard_map.76 = (f32[3,16,32,128]{3,2,1,0:T(8,128)S(1)}, f32[16,32,128]{2,1,0:T(8,128)S(1)}, f32[16,32,128]{2,1,0:T(8,128)S(1)}) custom-call(f32[3,16,32,128]{3,2,1,0:T(8,128)} %u_in.1, f32[3,16,32,128]{3,2,1,0:T(8,128)} %f_in.1, f32[16,32,128]{2,1,0:T(8,128)} %d_in.1, f32[16,32,128]{2,1,0:T(8,128)} %hist_in.1, s32[16,32,128]{2,1,0:T(8,128)} %crack_in.1), custom_call_target="tpu_custom_call" | custom-call | tf_op jit(solution)/shard_map/pallas_call | solution.py:472
  36.4 1.1 %shard_map.77 = (f32[3,16,32,128]{3,2,1,0:T(8,128)}, f32[16,32,128]{2,1,0:T(8,128)}, f32[16,32,128]{2,1,0:T(8,128)}) custom-call(f32[3,16,32,128]{3,2,1,0:T(8,128)S(1)} %get-tuple-element.6.u, f32[16,32,128]{2,1,0:T(8,128)S(1)} %get-tuple-element.7.d, f32[16,32,128]{2,1,0:T(8,128)S(1)} %get-tuple-element.8.h), custom_call_target="tpu_custom_call" | custom-call | tf_op jit(solution)/shard_map/pallas_call | solution.py:482
